TPU v7x, 128 devices: a whole 4x4x4 slice. The times are simulated.
128 devices in a mesh: row: 4 (over x_hi, core), col: 32 (over y, x_lo, z).
Axes of the slice: x: 4 (x_hi: 2, x_lo: 2; x = x_hi * 2 + x_lo), y: 4, z: 4, core: 2. Of those that a mesh axis runs over, the one named last changes fastest.
Arguments:
- tokens: bfloat16 [49152, 2048], P('col', 'row'), may hold values from -6 to 6
- in_weight: float32 [2048, 6144], P(('row', 'col')), may hold values from -0.125 to 0.125
- out_weight: float32 [2048, 2048], P(('row', 'col')), may hold values from -0.125 to 0.125
- beta_weight: float32 [2048, 16], replicated, may hold values from -0.25 to 0.25
- conv_weight: float32 [4, 6144], P(None, 'row'), may hold values from -2.5 to 2.5
- conv_prior: bfloat16 [96, 3, 6144], P('col', None, 'row'), may hold values from -6 to 6
- head_gain: float32 [2048], P('row'), may hold values from 0.1 to 1.9
- state_pool: float32 [192, 16, 128, 128], P('col', 'row'), may hold values from -2.5 to 2.5
- state_index: int32 [96, 16], P('col', 'row'), may hold values from 0 to 5
- lengths: int32 [96], P('col'), may hold values from 1 to 512, 36864 in all
- page_table: int32 [96, 4, 2], P('col'), may hold values from 0 to 31, as said below
Outputs:
- server_in: bfloat16 [2048, 6144], P('row', 'col')
- server_out: bfloat16 [2048, 2048], P('row', 'col')
- layer_out: bfloat16 [49152, 2048], P('col', 'row')
- final_state: float32 [96, 16, 128, 128], P('col', 'row')
- page_cache: bfloat16 [384, 128, 2, 2048], P('col', None, None, 'row')
Inputs may be any that keep to these rules, and one draw needn't show every extreme that they name: `lengths`: one prompt has all 512 tokens live. `state_index`: which of its own index of col's 6 stored states a prompt and head continues. page_table[p, g, 0] is the index of col that keeps page g of prompt p and page_table[p, g, 1] its slot there, below 12; every slot of every index of col gets exactly one page; the prompts of one index of col send at most 1 pages to any one index of col, and exactly 1 to some.
All inputs are finite; a program needn't handle non-finite values. No bound on the sum of `lengths` on one device may be relied on, other than what follows from the above.
Results may differ from a plain program's by a relative error of at most 0.029.
Values may be sent and summed in bfloat16 or wider, within the bound.
No kernel may reach another device: no remote copies, remote signals or barrier semaphores. Data moves between devices by JAX's collectives and lax.ppermute only.
A program may use at most 128 MiB of HBM per device.

v0:
```python
import jax
import jax.numpy as jnp
from jax import lax
from jax.sharding import PartitionSpec as P

DK = 128
STRETCH = 64
CONV = 4
SEQ = 512
PAGE = 128
PAGES_SEQ = 4
HIGHEST = lax.Precision.HIGHEST


def delta_block(carry_state, block_data):
    query_unit, key_unit, values, beta_rates = block_data
    width_c = beta_rates.shape[1]
    width_k = key_unit.shape[2]
    strict_lower = jnp.tril(jnp.ones((width_c, width_c), jnp.float32), -1)
    causal = jnp.tril(jnp.ones((width_c, width_c), jnp.float32))
    gram_matrix = jnp.einsum("bik,bjk->bij", key_unit, key_unit, precision=HIGHEST)
    system = (
        jnp.eye(width_c, dtype=jnp.float32) + beta_rates[:, :, None] * gram_matrix * strict_lower
    )
    right_side = jnp.concatenate([key_unit, values], axis=2) * beta_rates[:, :, None]
    solved = jax.scipy.linalg.solve_triangular(system, right_side, lower=True, unit_diagonal=True)
    weighted = solved[:, :, :width_k]
    corrected = solved[:, :, width_k:] - jnp.einsum(
        "bck,bkv->bcv", weighted, carry_state, precision=HIGHEST
    )
    scores = jnp.einsum("bik,bjk->bij", query_unit, key_unit, precision=HIGHEST) * causal
    output = jnp.einsum("bck,bkv->bcv", query_unit, carry_state, precision=HIGHEST) + jnp.einsum(
        "bij,bjv->biv", scores, corrected, precision=HIGHEST
    )
    carry_state = carry_state + jnp.einsum("bck,bcv->bkv", key_unit, corrected, precision=HIGHEST)
    return (carry_state, output)


def delta_scan(query_unit, key_unit, values, beta_rates, initial, block_len):
    batch_n = query_unit.shape[0]
    length_all = query_unit.shape[1]
    num_blocks = length_all // block_len

    def to_blocks(tensor):
        shaped = tensor.reshape((batch_n, num_blocks, block_len) + tensor.shape[2:])
        return jnp.moveaxis(shaped, 1, 0)

    last_state, outputs = lax.scan(
        delta_block,
        initial,
        (to_blocks(query_unit), to_blocks(key_unit), to_blocks(values), to_blocks(beta_rates)),
    )
    outputs = jnp.moveaxis(outputs, 0, 1).reshape(batch_n, length_all, -1)
    return (last_state, outputs)


def unit_rows(tensor):
    return tensor * lax.rsqrt(jnp.sum(tensor * tensor, axis=-1, keepdims=True) + 1e-06)


def local(
    tokens,
    in_weight,
    out_weight,
    beta_weight,
    conv_weight,
    conv_prior,
    head_gain,
    state_pool,
    state_index,
    lengths,
    page_table,
):
    row_count = lax.axis_size("row")
    col_count = lax.axis_size("col")
    row_id = lax.axis_index("row")
    local_tokens = tokens.shape[0]
    feature_span = tokens.shape[1]
    head_group = state_index.shape[1]
    head_width = 3 * DK
    prompts_here = lengths.shape[0]
    trainer_in = in_weight.astype(jnp.bfloat16)
    server_in, server_out = (
        lax.all_to_all(trainer_in, "col", split_axis=1, concat_axis=0, tiled=True),
        lax.all_to_all(
            out_weight.astype(jnp.bfloat16), "col", split_axis=1, concat_axis=0, tiled=True
        ),
    )
    beta_cast = beta_weight.astype(jnp.bfloat16)
    wide_in, wide_out = (
        lax.all_gather(server_in, "col", axis=1, tiled=True),
        lax.all_gather(server_out, "col", axis=1, tiled=True),
    )
    columns = wide_in
    product = jnp.dot(tokens, columns, preferred_element_type=jnp.float32)
    qkv_sum = lax.psum_scatter(
        product.reshape(local_tokens, lax.axis_size("row") * head_group, head_width)
        .transpose(1, 0, 2)
        .astype(jnp.bfloat16),
        "row",
        scatter_dimension=0,
        tiled=True,
    )
    beta_rows = lax.dynamic_slice_in_dim(beta_cast, row_id * feature_span, feature_span, 0)
    beta_term = jnp.dot(tokens, beta_rows, preferred_element_type=jnp.float32).T
    beta_sum = lax.psum_scatter(
        beta_term.astype(jnp.bfloat16), "row", scatter_dimension=0, tiled=True
    ).astype(jnp.float32)
    projected = qkv_sum.reshape(head_group, prompts_here, SEQ, head_width)
    prior_rows = conv_prior.reshape(prompts_here, CONV - 1, head_group, head_width).transpose(
        2, 0, 1, 3
    )
    padded = jnp.concatenate(
        [prior_rows.astype(jnp.float32), projected.astype(jnp.float32)], axis=2
    )
    taps_all = conv_weight.reshape(CONV, head_group, head_width)
    conv_sum = jnp.zeros(projected.shape, jnp.float32)
    for tap_id in range(CONV):
        conv_sum = (
            conv_sum + taps_all[tap_id][:, None, None, :] * padded[:, :, tap_id : tap_id + SEQ]
        )
    activated = jax.nn.silu(conv_sum).reshape(head_group * prompts_here, SEQ, 3, DK)
    query_unit = unit_rows(activated[:, :, 0])
    key_unit = unit_rows(activated[:, :, 1])
    values = activated[:, :, 2]
    live_mask = (jnp.arange(SEQ, dtype=jnp.int32)[None, :] < lengths[:, None]).astype(jnp.float32)
    live_batch = jnp.broadcast_to(live_mask[None], (head_group, prompts_here, SEQ)).reshape(
        head_group * prompts_here, SEQ
    )
    beta_rates = live_batch * jax.nn.sigmoid(beta_sum.reshape(head_group * prompts_here, SEQ))
    picked = state_pool[state_index, jnp.arange(head_group, dtype=jnp.int32)[None, :]]
    initial = picked.transpose(1, 0, 2, 3).reshape(head_group * prompts_here, DK, DK)
    last_state, outputs = delta_scan(query_unit, key_unit, values, beta_rates, initial, STRETCH)
    outputs = outputs * live_batch[:, :, None]
    normed = outputs.reshape(head_group, prompts_here, SEQ, DK)
    normed = (
        normed
        * lax.rsqrt(jnp.mean(normed * normed, axis=3, keepdims=True) + 1e-05)
        * head_gain.reshape(head_group, 1, 1, DK)
    )
    flat_heads = (
        normed.astype(jnp.bfloat16).transpose(1, 2, 0, 3).reshape(local_tokens, head_group * DK)
    )
    out_span = wide_out.shape[1] // row_count
    columns = wide_out
    product = jnp.dot(flat_heads, columns, preferred_element_type=jnp.float32)
    layer_out = (
        lax.psum_scatter(
            product.reshape(local_tokens, lax.axis_size("row") * 1, out_span)
            .transpose(1, 0, 2)
            .astype(jnp.bfloat16),
            "row",
            scatter_dimension=0,
            tiled=True,
        )
        .astype(jnp.float32)[0]
        .astype(jnp.bfloat16)
    )
    final_state = last_state.reshape(head_group, prompts_here, DK, DK).transpose(1, 0, 2, 3)
    keep_mask = live_batch[:, :, None]
    kept_pairs = jnp.stack([key_unit * keep_mask, values * keep_mask], axis=0).reshape(
        2, head_group, prompts_here, SEQ, DK
    )
    page_rows = (
        kept_pairs.transpose(2, 3, 0, 1, 4)
        .reshape(prompts_here * PAGES_SEQ, PAGE, 2, head_group * DK)
        .astype(jnp.bfloat16)
    )
    pages_dev = page_rows.shape[0]
    capacity = max(1, 2 * pages_dev // col_count)
    targets = page_table[:, :, 0].reshape(-1)
    slot_ids = page_table[:, :, 1].reshape(-1)
    order_ids = jnp.arange(pages_dev, dtype=jnp.int32)
    earlier = (targets[:, None] == targets[None, :]) & (order_ids[None, :] < order_ids[:, None])
    positions = targets * capacity + jnp.sum(earlier.astype(jnp.int32), axis=1)
    outgoing = (
        jnp.zeros((col_count * capacity,) + page_rows.shape[1:], jnp.bfloat16)
        .at[positions]
        .set(page_rows)
    )
    slot_send = jnp.full((col_count * capacity,), pages_dev, jnp.int32).at[positions].set(slot_ids)
    arrived, arrived_slots = (
        lax.all_to_all(outgoing, "col", split_axis=0, concat_axis=0, tiled=True),
        lax.all_to_all(slot_send, "col", split_axis=0, concat_axis=0, tiled=True),
    )
    page_cache = (
        jnp.zeros(page_rows.shape, jnp.bfloat16).at[arrived_slots].set(arrived, mode="drop")
    )
    return (server_in, server_out, layer_out, final_state, page_cache)


def solution(mesh):
    return jax.shard_map(
        local,
        mesh=mesh,
        in_specs=(
            P("col", "row"),
            P(("row", "col"), None),
            P(("row", "col"), None),
            P(),
            P(None, "row"),
            P("col", None, "row"),
            P("row"),
            P("col", "row", None, None),
            P("col", "row"),
            P("col"),
            P("col", None, None),
        ),
        out_specs=(
            P("row", "col"),
            P("row", "col"),
            P("col", "row"),
            P("col", "row", None, None),
            P("col", None, None, "row"),
        ),
        check_vma=False,
    )
```

profile of v0, /device:TPU:16, one launch (start us, length us, event | category | flops | bytes accessed | tf_op | source)
XLA Modules:
  0.0 1226.2 jit_solution(3627169898886624098)
XLA Ops:
  8.8 16.4 %all_to_all.55 = bf16[16,32,192]{2,0,1:T(8,128)(2,1)S(1)} all-to-all(bf16[16,32,192]{2,0,1:T(8,128)(2,1)S(1)} %copy.123), channel_id=1, replica_groups=mesh['row'=4,'col'=32] {'col'}, dimensions={1} | all-to-all | bytes 393216 | tf_op jit(solution)/shard_map/all_to_all | solution.py:84
  26.1 144.7 %all-gather.3.cloned.1.call-done = bf16[512,6144]{0,1:T(8,128)(2,1)} async-done(((bf16[512,192]{0,1:T(8,128)(2,1)}), bf16[512,6144]{0,1:T(8,128)(2,1)}) %all-gather.3.cloned.1.call-update) | async-done | bytes 6291472 | tf_op jit(solution)/shard_map/all_gather | solution.py:91
  170.8 15.9 %convolution_convert_fusion = bf16[1536,6144]{1,0:T(8,128)(2,1)} fusion(bf16[1536,512]{1,0:T(8,128)(2,1)S(1)} %copy-done, bf16[512,6144]{0,1:T(8,128)(2,1)} %all-gather.3.cloned.1.call-done), kind=kOutput, calls=%fused_computation.43 | convolution fusion | flops 9673113600 | bytes 26738688 | tf_op jit(solution)/shard_map/dot_general | solution.py:95
  186.7 18.3 %copy.164 = bf16[192,16,8,384]{3,2,0,1:T(8,128)(2,1)} copy(bf16[192,16,8,384]{3,2,1,0:T(8,128)(2,1)} %bitcast.161) | data formatting | bytes 37748736 | tf_op jit(solution)/shard_map/convert_element_type | solution.py:99
  207.0 25.2 %all-to-all-start.1 = ((bf16[32,2,512]{2,1,0:T(2,128)(2,1)}), bf16[32,2,512]{2,1,0:T(2,128)(2,1)S(1)}, u32[]{:S(2)}, u32[]{:S(2)}) async-start(bf16[32,2,512]{2,1,0:T(2,128)(2,1)} %reshape.338), calls=%async_computation.1 | async-start | bytes 131072 | tf_op jit(solution)/shard_map/all_to_all | solution.py:85
  234.8 13.6 %all-reduce = bf16[16,1536]{1,0:T(8,128)(2,1)S(1)} all-reduce(bf16[16,1536]{1,0:T(8,128)(2,1)S(1)} %convolution_convert_fusion.1), channel_id=3, replica_groups=mesh['row'=4,'col'=32] {'row'}, use_global_device_ids=true, to_apply=%region_3.4.clone | all-reduce | flops 24576 | bytes 98304
  252.5 116.9 %reduce-scatter.3.cloned.1.call-done = bf16[4,1536,384]{2,1,0:T(8,128)(2,1)} async-done(((bf16[16,1536,384]{2,1,0:T(8,128)(2,1)}), bf16[4,1536,384]{2,1,0:T(8,128)(2,1)}) %reduce-scatter.3.cloned.1.call-update) | async-done | bytes 4718608 | tf_op jit(solution)/shard_map/reduce_scatter | solution.py:96
  369.3 3.2 convert.14
  372.6 7.4 divide_multiply_fusion
  380.0 9.7 copy.129
  389.6 8.1 multiply_reduce_fusion
  397.8 3.5 copy.130
  401.4 3.6 copy.132
  405.0 3.6 copy.131
  408.6 3.8 multiply_bitcast_fusion.1
  414.5 554.7 %while.12 = (s32[]{:T(128)}, f32[12,128,128]{2,1,0:T(8,128)S(1)}, f32[8,12,64,128]{3,2,0,1:T(8,128)}, f32[8,12,64,128]{3,2,0,1:T(8,128)}, f32[8,12,64]{2,0,1:T(8...) while((s32[]{:T(128)}, f32[12,128,128]{2,1,0:T(8,128)S(1)}, ...), condition=%wide.region_5.6_spmd, body=%wide.region_4.5_spmd.sunk | while | flops 831590464 | bytes 12349789 | solution.py:48
  416.7 59.0 %custom-call.8 = f32[12,1,64,64]{2,3,1,0:T(8,128)S(1)} custom-call(f32[12,1,64,64]{3,2,1,0:T(8,128)S(1)} %fusion.93), custom_call_target="InvertDiagBlocksLowerTriangular" | custom-call | tf_op jit(solution)/shard_map/while/body/eval_jaxpr/jit(_solve_triangular)/vmap()/triangular_solve | solution.py:26
  479.8 2.6 fusion.97
  486.0 59.0 %custom-call.8 = f32[12,1,64,64]{2,3,1,0:T(8,128)S(1)} custom-call(f32[12,1,64,64]{3,2,1,0:T(8,128)S(1)} %fusion.93), custom_call_target="InvertDiagBlocksLowerTriangular" | custom-call | tf_op jit(solution)/shard_map/while/body/eval_jaxpr/jit(_solve_triangular)/vmap()/triangular_solve | solution.py:26
  549.1 2.6 fusion.97
  555.4 59.0 %custom-call.8 = f32[12,1,64,64]{2,3,1,0:T(8,128)S(1)} custom-call(f32[12,1,64,64]{3,2,1,0:T(8,128)S(1)} %fusion.93), custom_call_target="InvertDiagBlocksLowerTriangular" | custom-call | tf_op jit(solution)/shard_map/while/body/eval_jaxpr/jit(_solve_triangular)/vmap()/triangular_solve | solution.py:26
  618.5 2.6 fusion.97
  624.7 59.0 %custom-call.8 = f32[12,1,64,64]{2,3,1,0:T(8,128)S(1)} custom-call(f32[12,1,64,64]{3,2,1,0:T(8,128)S(1)} %fusion.93), custom_call_target="InvertDiagBlocksLowerTriangular" | custom-call | tf_op jit(solution)/shard_map/while/body/eval_jaxpr/jit(_solve_triangular)/vmap()/triangular_solve | solution.py:26
  687.8 2.6 fusion.97
  694.0 59.0 %custom-call.8 = f32[12,1,64,64]{2,3,1,0:T(8,128)S(1)} custom-call(f32[12,1,64,64]{3,2,1,0:T(8,128)S(1)} %fusion.93), custom_call_target="InvertDiagBlocksLowerTriangular" | custom-call | tf_op jit(solution)/shard_map/while/body/eval_jaxpr/jit(_solve_triangular)/vmap()/triangular_solve | solution.py:26
  757.1 2.6 fusion.97
  763.4 59.0 %custom-call.8 = f32[12,1,64,64]{2,3,1,0:T(8,128)S(1)} custom-call(f32[12,1,64,64]{3,2,1,0:T(8,128)S(1)} %fusion.93), custom_call_target="InvertDiagBlocksLowerTriangular" | custom-call | tf_op jit(solution)/shard_map/while/body/eval_jaxpr/jit(_solve_triangular)/vmap()/triangular_solve | solution.py:26
  826.5 2.6 fusion.97
  832.7 59.0 %custom-call.8 = f32[12,1,64,64]{2,3,1,0:T(8,128)S(1)} custom-call(f32[12,1,64,64]{3,2,1,0:T(8,128)S(1)} %fusion.93), custom_call_target="InvertDiagBlocksLowerTriangular" | custom-call | tf_op jit(solution)/shard_map/while/body/eval_jaxpr/jit(_solve_triangular)/vmap()/triangular_solve | solution.py:26
  895.8 2.6 fusion.97
  902.0 59.0 %custom-call.8 = f32[12,1,64,64]{2,3,1,0:T(8,128)S(1)} custom-call(f32[12,1,64,64]{3,2,1,0:T(8,128)S(1)} %fusion.93), custom_call_target="InvertDiagBlocksLowerTriangular" | custom-call | tf_op jit(solution)/shard_map/while/body/eval_jaxpr/jit(_solve_triangular)/vmap()/triangular_solve | solution.py:26
  965.1 2.6 fusion.97
  969.2 3.4 fusion.32
  972.8 2.6 fusion.33
  978.6 8.2 convert_bitcast_fusion
  989.3 7.6 all-to-all-start.2
  997.2 5.3 copy.142
  1002.5 4.9 copy.143
  1007.4 9.9 multiply_convert_fusion.1
  1017.4 3.9 maximum_bitcast_fusion
  1021.3 5.7 reshape.308
  1027.1 3.9 copy.144
  1030.9 4.2 broadcast_in_dim.32
  1035.1 8.4 scatter_fusion
  1043.5 8.3 all-to-all-start.3
  1053.5 139.6 %all-to-all-done.3 = bf16[32,128,2,512]{3,1,2,0:T(8,128)(2,1)} async-done(((bf16[32,128,2,512]{3,1,2,0:T(8,128)(2,1)}), bf16[32,128,2,512]{3,1,2,0:T(8,128)(2,1)}, u32[]{:S(2)}, u32[]{:S(2)}) %all-to-all-start.3) | async-done | bytes 8388640 | tf_op jit(solution)/shard_map/all_to_all | solution.py:183
  1195.2 17.7 %scatter_fusion.1 = bf16[12,128,2,512]{3,1,2,0:T(8,128)(2,1)} fusion(bf16[12,128,2,512]{3,1,2,0:T(8,128)(2,1)} %broadcast_in_dim.25, s32[32]{0:T(128)S(1)} %fusion.41, bf16[32,128,2,512]{3,1,2,0:T(8,128)(2,1)} %all-to-all-done.3), kind=kCustom, calls=%fused_computation.3 | custom fusion | bytes 25165952 | tf_op jit(solution)/shard_map/scatter | solution.py:187
  1212.8 6.8 copy.148
  (198 shorter events, 83.6 us)
Async XLA Ops:
  7.2 163.6 %copy-start = (bf16[1536,512]{1,0:T(8,128)(2,1)S(1)}, bf16[1536,512]{1,0:T(8,128)(2,1)}, u32[]{:S(2)}) copy-start(bf16[1536,512]{1,0:T(8,128)(2,1)} %param.13) | copy-start | bytes 4718596
  7.2 163.6 %all-gather.3.cloned.1.call-start = ((), (), s32[]{:S(2)}) async-start(), calls=%async_computation.6 | async-start | bytes 6488064 | tf_op jit(solution)/shard_map/all_gather | solution.py:91
  26.1 343.3 %reduce-scatter.3.cloned.1.call-start = ((), (), s32[]{:S(2)}) async-start(), calls=%async_computation.7 | async-start | bytes 23592960 | tf_op jit(solution)/shard_map/reduce_scatter | solution.py:96
  205.0 0.9 copy-start.3
  205.0 27.3 %copy-start.10 = (u32[128]{0:T(128)S(1)}, u32[128]{0:T(128)}, u32[]{:S(2)}) copy-start(u32[128]{0:T(128)} %constant.92) | copy-start | bytes 1540
  205.0 43.5 %copy-start.9 = (s32[3]{0:T(128)S(1)}, s32[3]{0:T(128)}, u32[]{:S(2)}) copy-start(s32[3]{0:T(128)} %param.22) | copy-start | bytes 40
  205.0 43.7 %copy-start.8 = (s32[3,4]{1,0:T(4,128)S(1)}, s32[3,4]{1,0:T(4,128)}, u32[]{:S(2)}) copy-start(s32[3,4]{1,0:T(4,128)} %param.21) | copy-start | bytes 148
  205.9 42.9 %copy-start.5 = (f32[4,1536]{1,0:T(4,128)S(1)}, f32[4,1536]{1,0:T(4,128)}, u32[]{:S(2)}) copy-start(f32[4,1536]{1,0:T(4,128)} %param.17) | copy-start | bytes 73732
  205.9 43.0 %copy-start.4 = (bf16[3,3,1536]{2,1,0:T(4,128)(2,1)S(1)}, bf16[3,3,1536]{2,1,0:T(4,128)(2,1)}, u32[]{:S(2)}) copy-start(bf16[3,3,1536]{2,1,0:T(4,128)(2,1)} %param.18) | copy-start | bytes 82948
  207.0 44.6 %all-to-all-start.1 = ((bf16[32,2,512]{2,1,0:T(2,128)(2,1)}), bf16[32,2,512]{2,1,0:T(2,128)(2,1)S(1)}, u32[]{:S(2)}, u32[]{:S(2)}) async-start(bf16[32,2,512]{2,1,0:T(2,128)(2,1)} %reshape.338), calls=%async_computation.1 | async-start | bytes 131072 | tf_op jit(solution)/shard_map/all_to_all | solution.py:85
  232.2 746.4 %all-gather.5.cloned.1.call-start = ((), (), s32[]{:S(2)}) async-start(), calls=%async_computation.8 | async-start | bytes 2162688 | tf_op jit(solution)/shard_map/all_gather | solution.py:92
  252.4 967.2 %reduce-scatter.5.cloned.1.call-start = ((), (), s32[]{:S(2)}) async-start(), calls=%async_computation.9 | async-start | bytes 7864320 | tf_op jit(solution)/shard_map/reduce_scatter | solution.py:148
  408.6 3.8 copy-start.2
  969.2 3.6 copy-start.7
  986.8 0.7 copy-start.6
  989.3 54.2 %all-to-all-start.2 = ((s32[32,1,1]{2,1,0:T(1,128)}), s32[32,1,1]{2,1,0:T(1,128)S(1)}, u32[]{:S(2)}, u32[]{:S(2)}) async-start(s32[32,1,1]{2,1,0:T(1,128)} %copy.140), calls=%async_computation.4 | async-start | bytes 32768 | tf_op jit(solution)/shard_map/all_to_all | solution.py:184
  1043.5 149.6 %all-to-all-start.3 = ((bf16[32,128,2,512]{3,1,2,0:T(8,128)(2,1)}), bf16[32,128,2,512]{3,1,2,0:T(8,128)(2,1)}, u32[]{:S(2)}, u32[]{:S(2)}) async-start(bf16[32,128,2,512]{3,1,2,0:T(8,128)(2,1)} %scatter_fusion), calls=%async_computation.5 | async-start | bytes 16777216 | tf_op jit(solution)/shard_map/all_to_all | solution.py:183
  1195.2 24.5 %copy-start.1 = (bf16[1536,512]{1,0:T(8,128)(2,1)S(1)}, bf16[1536,512]{1,0:T(8,128)(2,1)}, u32[]{:S(2)}) copy-start(bf16[1536,512]{1,0:T(8,128)(2,1)} %param.13) | copy-start | bytes 4718596
Sparse Core Ops, SparseCore 0:
  26.2 144.5 all-gather.2
  205.2 164.0 reduce-scatter.2
  371.7 135.9 all-gather.4
  987.0 64.7 reduce-scatter.4
where the time goes:
time: 1230 us
  other arithmetic  520 us (42%)
  waiting for transfers between devices  401 us (33%)
  local copies, waits for them, and re-layouts  122 us (10%)
  matrix products  96.3 us (8%)
  starting transfers between devices  41.4 us (3%)
  blocking collectives  30 us (2%)
  between operations  14.8 us (1%)
    another operation x32, other arithmetic, delta_block(): jax.scipy.linalg.solve_triangular(system, right_side, lower=True, unit_di...  473 us
    all_gather x1, waiting for transfers between devices, local(): lax.all_gather(server_in, 'col', axis=1, tiled=True)  145 us
    all_to_all x1, waiting for transfers between devices, local(): lax.all_to_all(outgoing, 'col', split_axis=0, concat_axis=0, tiled=True)  140 us
    reduce_scatter x1, waiting for transfers between devices, local(): lax.psum_scatter(product.reshape(local_tokens, lax.axis_size('row') * hea...  117 us
    all_to_all x1, starting transfers between devices, local(): lax.all_to_all(out_weight.astype(jnp.bfloat16), 'col', split_axis=1, conc...  25.2 us
  transfers between devices with their start and end apart: 7, of which 3 were waited for; matrix products, arithmetic and copies ran while one was open for 56% of the time, Pallas kernels for 0%

commit v1 on v0

--- a/solution.py
+++ b/solution.py
@@ -88,7 +88,9 @@
     )
     beta_cast = beta_weight.astype(jnp.bfloat16)
     wide_in, wide_out = (
-        lax.all_gather(server_in, "col", axis=1, tiled=True),
+        jnp.concatenate(
+            lax.all_to_all(jnp.stack([server_in] * lax.axis_size("col")), "col", 0, 0), axis=1
+        ),
         lax.all_gather(server_out, "col", axis=1, tiled=True),
     )
     columns = wide_in

time: 1230 us -> 1130 us (0.919)
  waiting for transfers between devices: 401 us -> 255 us
  blocking collectives: 30 us -> 107 us
  local copies, waits for them, and re-layouts: 122 us -> 103 us
  starting transfers between devices: 41.4 us -> 22.8 us
    all_gather x1 -> x0, waiting for transfers between devices: 145 us -> none  [local(): lax.all_gather(server_in, 'col', axis=1, tiled=True)]
    all_to_all x0 -> x1, blocking collectives: none -> 75.7 us  [local(): lax.all_to_all(jnp.stack([server_in] * lax.axis_size('col')), 'col', 0, 0)]
    all_to_all x1, starting transfers between devices: 25.2 us -> 6.31 us  [local(): lax.all_to_all(out_weight.astype(jnp.bfloat16), 'col', split_axis=1, conc...]
  transfers between devices with their start and end apart: 7 -> 6, of which waited for: 3 -> 2; matrix products, arithmetic and copies ran while one was open for 56% -> 62% of each run, Pallas kernels for 0% -> 0%
where the time goes in v1:
time: 1130 us; the launch traced here: 1120 us
  other arithmetic  523 us (46%)
  waiting for transfers between devices  255 us (23%)
  blocking collectives  107 us (9%)
  local copies, waits for them, and re-layouts  103 us (9%)
  matrix products  96.3 us (9%)
  starting transfers between devices  22.8 us (2%)
  between operations  16.8 us (1%)
    another operation x32, other arithmetic, delta_block(): jax.scipy.linalg.solve_triangular(system, right_side, lower=True, unit_di...  473 us
    all_to_all x1, waiting for transfers between devices, local(): lax.all_to_all(outgoing, 'col', split_axis=0, concat_axis=0, tiled=True)  136 us
    reduce_scatter x1, waiting for transfers between devices, local(): lax.psum_scatter(product.reshape(local_tokens, lax.axis_size('row') * hea...  119 us
    all_to_all x1, blocking collectives, local(): lax.all_to_all(jnp.stack([server_in] * lax.axis_size('col')), 'col', 0, 0)  75.7 us
  transfers between devices with their start and end apart: 6, of which 2 were waited for; matrix products, arithmetic and copies ran while one was open for 62% of the time, Pallas kernels for 0%

profile of v1, /device:TPU:16, one launch (start us, length us, event | category | flops | bytes accessed | tf_op | source)
XLA Modules:
  0.0 1124.4 jit_solution(16898260078840495810)
XLA Ops:
  9.7 16.4 %all_to_all.60 = bf16[16,32,192]{2,0,1:T(8,128)(2,1)S(1)} all-to-all(bf16[16,32,192]{2,0,1:T(8,128)(2,1)S(1)} %copy.128), channel_id=1, replica_groups=mesh['row'=4,'col'=32] {'col'}, dimensions={1} | all-to-all | bytes 393216 | tf_op jit(solution)/shard_map/all_to_all | solution.py:84
  26.9 75.7 %all_to_all.61 = bf16[32,512,192]{1,2,0:T(8,128)(2,1)} all-to-all(bf16[32,512,192]{1,2,0:T(8,128)(2,1)S(1)} %stack.4), channel_id=1, replica_groups=mesh['row'=4,'col'=32] {'col'}, dimensions={0} | all-to-all | bytes 12582912 | tf_op jit(solution)/shard_map/all_to_all | solution.py:92
  102.6 15.9 %convert_bitcast_fusion = bf16[16,1536,384]{2,1,0:T(8,128)(2,1)} fusion(bf16[16,384,512]{2,1,0:T(8,128)(2,1)} %bitcast.168, bf16[1536,512]{1,0:T(8,128)(2,1)S(1)} %copy-done), kind=kOutput, calls=%fused_computation.43 | convolution fusion | flops 9673113600 | bytes 26738688 | tf_op jit(solution)/shard_map/dot_general | solution.py:97
  120.4 6.3 all-to-all-start.1
  129.3 14.6 %all-reduce = bf16[16,1536]{1,0:T(8,128)(2,1)S(1)} all-reduce(bf16[16,1536]{1,0:T(8,128)(2,1)S(1)} %convolution_convert_fusion), channel_id=3, replica_groups=mesh['row'=4,'col'=32] {'row'}, use_global_device_ids=true, to_apply=%region_3.4.clone | all-reduce | flops 24576 | bytes 98304
  144.4 2.2 copy.132
  150.1 118.6 %reduce-scatter.3.cloned.1.call-done = bf16[4,1536,384]{2,1,0:T(8,128)(2,1)} async-done(((bf16[16,1536,384]{2,1,0:T(8,128)(2,1)}), bf16[4,1536,384]{2,1,0:T(8,128)(2,1)}) %reduce-scatter.3.cloned.1.call-update) | async-done | bytes 4718608 | tf_op jit(solution)/shard_map/reduce_scatter | solution.py:98
  268.8 7.5 copy.133
  276.3 17.4 %divide_multiply_fusion = f32[4,3,512,384]{2,3,1,0:T(8,128)S(1)} fusion(f32[4,3,512,384]{2,3,1,0:T(8,128)} %copy.133, f32[4,3,3,384]{2,3,1,0:T(8,128)} %copy.132, f32[4,384]{1,0:T(4,128)S(1)} %mul.198, f32[4,384]{1,0:T(4,128)S(1)} %mul.195, f32[4,384]{1,0:T(4,128)S(1)} %mul.192, f32[4,384]{1,0:T(4,128)S(1)} %mul.189), kind=kLoop, calls=%fused_computation.57 | loop fusion | flops 33030144 | bytes 18954240 | tf_op jit(solution)/shard_map/jit(silu)/mul | solution.py:124
  293.7 4.1 multiply_reduce_fusion
  297.9 3.5 copy.135
  301.5 3.6 copy.137
  305.1 3.6 copy.136
  308.6 3.8 multiply_bitcast_fusion.1
  314.5 555.2 %while.12 = (s32[]{:T(128)}, f32[12,128,128]{2,1,0:T(8,128)S(1)}, f32[8,12,64,128]{3,2,0,1:T(8,128)}, f32[8,12,64,128]{3,2,0,1:T(8,128)}, f32[8,12,64]{2,0,1:T(8...) while((s32[]{:T(128)}, f32[12,128,128]{2,1,0:T(8,128)S(1)}, ...), condition=%wide.region_5.6_spmd, body=%wide.region_4.5_spmd.sunk | while | flops 831590464 | bytes 12349789 | solution.py:48
  317.2 59.0 %custom-call.8 = f32[12,1,64,64]{2,3,1,0:T(8,128)S(1)} custom-call(f32[12,1,64,64]{3,2,1,0:T(8,128)S(1)} %fusion.93), custom_call_target="InvertDiagBlocksLowerTriangular" | custom-call | tf_op jit(solution)/shard_map/while/body/eval_jaxpr/jit(_solve_triangular)/vmap()/triangular_solve | solution.py:26
  380.3 2.6 fusion.97
  386.5 59.0 %custom-call.8 = f32[12,1,64,64]{2,3,1,0:T(8,128)S(1)} custom-call(f32[12,1,64,64]{3,2,1,0:T(8,128)S(1)} %fusion.93), custom_call_target="InvertDiagBlocksLowerTriangular" | custom-call | tf_op jit(solution)/shard_map/while/body/eval_jaxpr/jit(_solve_triangular)/vmap()/triangular_solve | solution.py:26
  449.7 2.6 fusion.97
  455.9 59.0 %custom-call.8 = f32[12,1,64,64]{2,3,1,0:T(8,128)S(1)} custom-call(f32[12,1,64,64]{3,2,1,0:T(8,128)S(1)} %fusion.93), custom_call_target="InvertDiagBlocksLowerTriangular" | custom-call | tf_op jit(solution)/shard_map/while/body/eval_jaxpr/jit(_solve_triangular)/vmap()/triangular_solve | solution.py:26
  519.0 2.6 fusion.97
  525.2 59.0 %custom-call.8 = f32[12,1,64,64]{2,3,1,0:T(8,128)S(1)} custom-call(f32[12,1,64,64]{3,2,1,0:T(8,128)S(1)} %fusion.93), custom_call_target="InvertDiagBlocksLowerTriangular" | custom-call | tf_op jit(solution)/shard_map/while/body/eval_jaxpr/jit(_solve_triangular)/vmap()/triangular_solve | solution.py:26
  588.3 2.6 fusion.97
  594.5 59.0 %custom-call.8 = f32[12,1,64,64]{2,3,1,0:T(8,128)S(1)} custom-call(f32[12,1,64,64]{3,2,1,0:T(8,128)S(1)} %fusion.93), custom_call_target="InvertDiagBlocksLowerTriangular" | custom-call | tf_op jit(solution)/shard_map/while/body/eval_jaxpr/jit(_solve_triangular)/vmap()/triangular_solve | solution.py:26
  657.7 2.6 fusion.97
  663.9 59.0 %custom-call.8 = f32[12,1,64,64]{2,3,1,0:T(8,128)S(1)} custom-call(f32[12,1,64,64]{3,2,1,0:T(8,128)S(1)} %fusion.93), custom_call_target="InvertDiagBlocksLowerTriangular" | custom-call | tf_op jit(solution)/shard_map/while/body/eval_jaxpr/jit(_solve_triangular)/vmap()/triangular_solve | solution.py:26
  727.0 2.6 fusion.97
  733.2 59.0 %custom-call.8 = f32[12,1,64,64]{2,3,1,0:T(8,128)S(1)} custom-call(f32[12,1,64,64]{3,2,1,0:T(8,128)S(1)} %fusion.93), custom_call_target="InvertDiagBlocksLowerTriangular" | custom-call | tf_op jit(solution)/shard_map/while/body/eval_jaxpr/jit(_solve_triangular)/vmap()/triangular_solve | solution.py:26
  796.3 2.6 fusion.97
  802.5 59.0 %custom-call.8 = f32[12,1,64,64]{2,3,1,0:T(8,128)S(1)} custom-call(f32[12,1,64,64]{3,2,1,0:T(8,128)S(1)} %fusion.93), custom_call_target="InvertDiagBlocksLowerTriangular" | custom-call | tf_op jit(solution)/shard_map/while/body/eval_jaxpr/jit(_solve_triangular)/vmap()/triangular_solve | solution.py:26
  865.7 2.6 fusion.97
  869.7 3.2 fusion.32
  873.1 2.6 fusion.33
  876.9 2.1 reshape.337
  879.1 8.2 convert_bitcast_fusion.1
  889.8 7.4 all-to-all-start.3
  897.5 5.2 copy.147
  902.7 5.0 copy.148
  907.6 9.9 multiply_convert_fusion.1
  917.6 3.9 maximum_bitcast_fusion
  921.5 5.7 reshape.319
  927.3 3.9 copy.149
  931.1 4.2 broadcast_in_dim.32
  935.4 8.4 scatter_fusion
  943.7 8.7 all-to-all-start.4
  954.1 136.0 %all-to-all-done.4 = bf16[32,128,2,512]{3,1,2,0:T(8,128)(2,1)} async-done(((bf16[32,128,2,512]{3,1,2,0:T(8,128)(2,1)}), bf16[32,128,2,512]{3,1,2,0:T(8,128)(2,1)}, u32[]{:S(2)}, u32[]{:S(2)}) %all-to-all-start.4) | async-done | bytes 8388640 | tf_op jit(solution)/shard_map/all_to_all | solution.py:185
  1092.2 17.7 %scatter_fusion.1 = bf16[12,128,2,512]{3,1,2,0:T(8,128)(2,1)} fusion(bf16[12,128,2,512]{3,1,2,0:T(8,128)(2,1)} %broadcast_in_dim.25, s32[32]{0:T(128)S(1)} %fusion.42, bf16[32,128,2,512]{3,1,2,0:T(8,128)(2,1)} %all-to-all-done.4), kind=kCustom, calls=%fused_computation.3 | custom fusion | bytes 25165952 | tf_op jit(solution)/shard_map/scatter | solution.py:189
  1109.9 6.8 copy.153
  (197 shorter events, 81.6 us)
Async XLA Ops:
  8.0 94.6 %copy-start = (bf16[1536,512]{1,0:T(8,128)(2,1)S(1)}, bf16[1536,512]{1,0:T(8,128)(2,1)}, u32[]{:S(2)}) copy-start(bf16[1536,512]{1,0:T(8,128)(2,1)} %param.13) | copy-start | bytes 4718596
  8.0 260.8 %reduce-scatter.3.cloned.1.call-start = ((), (), s32[]{:S(2)}) async-start(), calls=%async_computation.7 | async-start | bytes 23592960 | tf_op jit(solution)/shard_map/reduce_scatter | solution.py:98
  26.2 0.7 copy-start.3
  118.5 0.9 copy-start.4
  118.5 8.3 copy-start.11
  118.5 25.6 %copy-start.10 = (s32[3]{0:T(128)S(1)}, s32[3]{0:T(128)}, u32[]{:S(2)}) copy-start(s32[3]{0:T(128)} %param.22) | copy-start | bytes 40
  118.5 25.7 %copy-start.9 = (s32[3,4]{1,0:T(4,128)S(1)}, s32[3,4]{1,0:T(4,128)}, u32[]{:S(2)}) copy-start(s32[3,4]{1,0:T(4,128)} %param.21) | copy-start | bytes 148
  119.4 24.9 %copy-start.6 = (f32[4,1536]{1,0:T(4,128)S(1)}, f32[4,1536]{1,0:T(4,128)}, u32[]{:S(2)}) copy-start(f32[4,1536]{1,0:T(4,128)} %param.17) | copy-start | bytes 73732
  119.4 25.0 %copy-start.5 = (bf16[3,3,1536]{2,1,0:T(4,128)(2,1)S(1)}, bf16[3,3,1536]{2,1,0:T(4,128)(2,1)}, u32[]{:S(2)}) copy-start(bf16[3,3,1536]{2,1,0:T(4,128)(2,1)} %param.18) | copy-start | bytes 82948
  120.4 28.5 %all-to-all-start.1 = ((bf16[32,2,512]{2,1,0:T(2,128)(2,1)}), bf16[32,2,512]{2,1,0:T(2,128)(2,1)S(1)}, u32[]{:S(2)}, u32[]{:S(2)}) async-start(bf16[32,2,512]{2,1,0:T(2,128)(2,1)} %reshape.350), calls=%async_computation.1 | async-start | bytes 131072 | tf_op jit(solution)/shard_map/all_to_all | solution.py:85
  126.7 752.4 %all-gather.2.cloned.1.call-start = ((), (), s32[]{:S(2)}) async-start(), calls=%async_computation.8 | async-start | bytes 2162688 | tf_op jit(solution)/shard_map/all_gather | solution.py:94
  149.8 966.9 %reduce-scatter.5.cloned.1.call-start = ((), (), s32[]{:S(2)}) async-start(), calls=%async_computation.9 | async-start | bytes 7864320 | tf_op jit(solution)/shard_map/reduce_scatter | solution.py:150
  308.6 3.8 copy-start.2
  869.7 3.4 copy-start.8
  887.3 0.7 copy-start.7
  889.8 54.0 %all-to-all-start.3 = ((s32[32,1,1]{2,1,0:T(1,128)}), s32[32,1,1]{2,1,0:T(1,128)S(1)}, u32[]{:S(2)}, u32[]{:S(2)}) async-start(s32[32,1,1]{2,1,0:T(1,128)} %copy.145), calls=%async_computation.5 | async-start | bytes 32768 | tf_op jit(solution)/shard_map/all_to_all | solution.py:186
  943.7 146.4 %all-to-all-start.4 = ((bf16[32,128,2,512]{3,1,2,0:T(8,128)(2,1)}), bf16[32,128,2,512]{3,1,2,0:T(8,128)(2,1)}, u32[]{:S(2)}, u32[]{:S(2)}) async-start(bf16[32,128,2,512]{3,1,2,0:T(8,128)(2,1)} %scatter_fusion), calls=%async_computation.6 | async-start | bytes 16777216 | tf_op jit(solution)/shard_map/all_to_all | solution.py:185
  1092.2 24.5 %copy-start.1 = (bf16[1536,512]{1,0:T(8,128)(2,1)S(1)}, bf16[1536,512]{1,0:T(8,128)(2,1)}, u32[]{:S(2)}) copy-start(bf16[1536,512]{1,0:T(8,128)(2,1)} %param.13) | copy-start | bytes 4718596
Sparse Core Ops, SparseCore 0:
  118.6 150.0 reduce-scatter.2
  887.4 64.4 reduce-scatter.4
Sparse Core Ops, SparseCore 1:
  149.9 221.0 all-gather.1
